TPU v7x, 32 devices: a whole 2x2x4 slice. The times are simulated.
32 devices in a mesh: pb: 8 (over z, y), ka: 4 (over x, core).
Axes of the slice: x: 2, y: 2, z: 4, core: 2. Of those that a mesh axis runs over, the one named last changes fastest.
Arguments:
- pair_trunk: bfloat16 [384, 384, 128], P('pb', 'ka'), may hold values from -40 to 40
- token_ids: int32 [3, 384], replicated, may hold values from 0 to 422, as said below
- w_rel: bfloat16 [139, 128], replicated, may hold values from -3.5 to 3.5
- cat_gain: float32 [256], replicated, may hold values from 0.1 to 1.9
- w_in: bfloat16 [256, 128], replicated, may hold values from -0.375 to 0.375
- trans_gain: float32 [2, 128], replicated, may hold values from 0.1 to 1.9
- trans_ab: bfloat16 [2, 128, 512], replicated, may hold values from -0.5 to 0.5
- trans_out: bfloat16 [2, 256, 128], replicated, may hold values from -0.375 to 0.375
- bias_gain: float32 [128], replicated, may hold values from 0.1 to 1.9
- w_bias: bfloat16 [128, 16], replicated, may hold values from -1.5 to 1.5
- normed: bfloat16 [8, 384, 768], P(None, 'pb', 'ka'), may hold values from -12 to 12
- w_proj: bfloat16 [4, 768, 768], P(None, None, 'ka'), may hold values from -1 to 1
- output_weight: bfloat16 [768, 768], P('ka'), may hold values from -0.21875 to 0.21875
Outputs:
- pair_cond: bfloat16 [384, 384, 128], P('pb', 'ka')
- update: bfloat16 [8, 384, 768], P(None, 'pb', 'ka')
Inputs may be any that keep to these rules, and one draw needn't show every extreme that they name: `token_ids`: row 0 is a token's residue number, row 1 its chain number, row 2 its entity number. Chain numbers start at 0 and never fall along the tokens; residue numbers never fall within a chain; all tokens of a chain share one entity. The last token's residue number is 422.
All inputs are finite; a program needn't handle non-finite values.
Results may differ from a plain program's by a relative error of at most 0.015.
The roundings to bfloat16 on the way count: a program that leaves them out, or rounds other values in their place, can miss the bound.
Values may be sent and summed in bfloat16 or wider, within the bound.
A program may use at most 64 MiB of HBM per device.

v0:
```python
import math
import jax
import jax.numpy as jnp
from jax import lax
from jax.sharding import PartitionSpec as P

HD = 48
RMAX = 32
SMAX = 2
REL = 139
EPS = 1e-05


def layer_norm(values, scaling):
    average = jnp.mean(values, axis=-1, keepdims=True)
    centered = values - average
    spread = jnp.mean(centered * centered, axis=-1, keepdims=True)
    return centered * lax.rsqrt(spread + EPS) * scaling


def relative_onehot(query_token_ids, key_ids, query_pos, key_pos):
    query_res = query_token_ids[0][:, None]
    key_res = key_ids[0][None, :]
    query_chain = query_token_ids[1][:, None]
    key_chain = key_ids[1][None, :]
    query_entity = query_token_ids[2][:, None]
    key_ent = key_ids[2][None, :]
    same_chain = query_chain == key_chain
    same_res = same_chain & (query_res == key_res)
    same_entity = query_entity == key_ent
    res_bins = 2 * RMAX + 2
    res_bin = jnp.where(same_chain, jnp.clip(query_res - key_res + RMAX, 0, 2 * RMAX), 2 * RMAX + 1)
    token_offset_bin = jnp.where(
        same_res, jnp.clip(query_pos[:, None] - key_pos[None, :] + RMAX, 0, 2 * RMAX), 2 * RMAX + 1
    )
    chain_offset_bin = jnp.where(
        same_entity, jnp.clip(query_chain - key_chain + SMAX, 0, 2 * SMAX), 2 * SMAX + 1
    )
    columns = jnp.arange(REL, dtype=jnp.int32)
    onehot = (columns == res_bin[..., None]) | (columns == (res_bins + token_offset_bin)[..., None])
    onehot = onehot | (columns == (2 * res_bins + chain_offset_bin)[..., None])
    onehot = onehot | (columns == REL - 1) & same_entity[..., None]
    return onehot.astype(jnp.bfloat16)


def condition_block(
    trunk_blk, onehot, w_rel, cat_gain, w_in, trans_gain, trans_ab, trans_out, bias_gain, w_bias
):
    half = trans_out.shape[1]
    relative = jnp.einsum("rkf,fc->rkc", onehot, w_rel, preferred_element_type=jnp.float32)
    joined = jnp.concatenate([trunk_blk.astype(jnp.float32), relative], axis=-1)
    normal_in = layer_norm(joined, cat_gain).astype(jnp.bfloat16)
    pair_state = jnp.einsum("rkf,fc->rkc", normal_in, w_in, preferred_element_type=jnp.float32)
    for layer_idx in range(2):
        normal_tr = layer_norm(pair_state, trans_gain[layer_idx]).astype(jnp.bfloat16)
        gate_up = jnp.einsum(
            "rkc,cf->rkf", normal_tr, trans_ab[layer_idx], preferred_element_type=jnp.float32
        )
        hidden = (jax.nn.silu(gate_up[..., :half]) * gate_up[..., half:]).astype(jnp.bfloat16)
        pair_state = pair_state + jnp.einsum(
            "rkf,fc->rkc", hidden, trans_out[layer_idx], preferred_element_type=jnp.float32
        )
    normal_b = layer_norm(pair_state, bias_gain).astype(jnp.bfloat16)
    bias_blk = jnp.einsum(
        "rkc,ch->hrk", normal_b, w_bias, preferred_element_type=jnp.float32
    ).astype(jnp.bfloat16)
    return (pair_state.astype(jnp.bfloat16), bias_blk)


def soft_weights(logits):
    row_max = jnp.max(logits, axis=-1, keepdims=True)
    expweights = jnp.exp(logits - row_max)
    return (expweights / jnp.sum(expweights, axis=-1, keepdims=True)).astype(jnp.bfloat16)


def shards(
    pair_trunk,
    token_ids,
    w_rel,
    cat_gain,
    w_in,
    trans_gain,
    trans_ab,
    trans_out,
    bias_gain,
    w_bias,
    normed,
    w_proj,
    output_weight,
):
    q_rows = pair_trunk.shape[0]
    k_rows = pair_trunk.shape[1]
    q_start = lax.axis_index("pb") * q_rows
    k_start = lax.axis_index("ka") * k_rows
    key_ids = lax.dynamic_slice_in_dim(token_ids, k_start, k_rows, 1)
    key_pos = k_start + jnp.arange(k_rows, dtype=jnp.int32)
    row_blk = 8

    def one_block(block_idx):
        begin_at = block_idx * row_blk
        trunk_blk = lax.dynamic_slice_in_dim(pair_trunk, begin_at, row_blk, 0)
        query_token_ids = lax.dynamic_slice_in_dim(token_ids, q_start + begin_at, row_blk, 1)
        query_pos = q_start + begin_at + jnp.arange(row_blk, dtype=jnp.int32)
        onehot = relative_onehot(query_token_ids, key_ids, query_pos, key_pos)
        return condition_block(
            trunk_blk,
            onehot,
            w_rel,
            cat_gain,
            w_in,
            trans_gain,
            trans_ab,
            trans_out,
            bias_gain,
            w_bias,
        )

    pair_blocks, bias_blocks = lax.map(one_block, jnp.arange(q_rows // row_blk, dtype=jnp.int32))
    pair_cond = pair_blocks.reshape(q_rows, k_rows, pair_blocks.shape[-1])
    bias_tile = jnp.transpose(bias_blocks, (1, 0, 2, 3)).reshape(
        bias_blocks.shape[1], q_rows, k_rows
    )
    samples = normed.shape[0]
    feat_local = normed.shape[2]
    heads_local = feat_local // HD
    scale_factor = 1.0 / math.sqrt(HD)
    projected = jnp.einsum(
        "sqf,pfe->psqe",
        lax.all_gather(normed, "ka", axis=2, tiled=True),
        w_proj,
        preferred_element_type=jnp.float32,
    )
    queries = projected[0].astype(jnp.bfloat16).reshape(samples, q_rows, heads_local, HD)
    kv_local = jnp.transpose(
        jnp.stack([projected[1], projected[2]], axis=1).astype(jnp.bfloat16), (0, 1, 3, 2)
    )
    bias_rows = lax.all_to_all(bias_tile, "ka", split_axis=0, concat_axis=2, tiled=True)
    kv_all = lax.all_gather(kv_local, "pb", axis=3, tiled=True)
    keys_all = kv_all[:, 0].reshape(samples, heads_local, HD, kv_all.shape[3])
    values_all = kv_all[:, 1].reshape(samples, heads_local, HD, kv_all.shape[3])
    logits = (
        jnp.einsum("sqhd,shdk->shqk", queries, keys_all, preferred_element_type=jnp.float32)
        * scale_factor
    )
    logits = logits + bias_rows[None].astype(jnp.float32)
    weights = soft_weights(logits)
    attended = jnp.einsum(
        "shqk,shdk->sqhd", weights, values_all, preferred_element_type=jnp.float32
    )
    gated_result = (
        attended.reshape(samples, q_rows, feat_local) * jax.nn.sigmoid(projected[3])
    ).astype(jnp.bfloat16)
    flat_gated = gated_result.reshape(samples * q_rows, feat_local)
    summed = lax.psum_scatter(
        jnp.einsum(
            "fe,nf->en", output_weight, flat_gated, preferred_element_type=jnp.float32
        ).astype(jnp.bfloat16),
        "ka",
        scatter_dimension=0,
        tiled=True,
    ).astype(jnp.float32)
    update = jnp.transpose(summed).reshape(samples, q_rows, feat_local).astype(jnp.bfloat16)
    return (pair_cond, update)


def solution(mesh):
    in_specs = (
        P("pb", "ka", None),
        P(),
        P(),
        P(),
        P(),
        P(),
        P(),
        P(),
        P(),
        P(),
        P(None, "pb", "ka"),
        P(None, None, "ka"),
        P("ka", None),
    )
    out_specs = (P("pb", "ka", None), P(None, "pb", "ka"))
    return jax.shard_map(shards, mesh=mesh, in_specs=in_specs, out_specs=out_specs, check_vma=False)
```

profile of v0, /device:TPU:0, one launch (start us, length us, event | category | flops | bytes accessed | tf_op | source)
XLA Modules:
  0.0 148.7 jit_solution(9345763957200801556)
XLA Ops:
  7.2 1.3 copy.25
  8.5 14.3 %all_gather.6 = bf16[8,48,768]{1,0,2:T(8,128)(2,1)S(1)} all-gather(bf16[8,48,192]{1,0,2:T(8,128)(2,1)S(1)} %copy.25), channel_id=1, replica_groups=mesh['pb'=8,'ka'=4] {'ka'}, dimensions={2}, use_global_device_ids=true | all-gather | bytes 737280 | tf_op jit(solution)/shard_map/all_gather | solution.py:129
  22.8 1.6 %copy.26 = bf16[8,48,768]{2,1,0:T(8,128)(2,1)} copy(bf16[8,48,768]{1,0,2:T(8,128)(2,1)S(1)} %all_gather.6) | data formatting | bytes 1179648 | tf_op jit(solution)/shard_map/all_gather | solution.py:129
  24.5 1.8 %fusion.70 = (bf16[4,8,48,192]{3,2,1,0:T(8,128)(2,1)S(1)}, f32[4,8,48,192]{3,2,1,0:T(8,128)S(1)}) fusion(bf16[8,48,768]{2,1,0:T(8,128)(2,1)} %copy.26, bf16[4,768,192]{1,2,0:T(8,128)(2,1)S(1)} %copy-done), kind=kOutput, calls=%fused_computation.118 | convolution fusion | flops 453279744 | bytes 3538944 | tf_op jit(solution)/shard_map/sqf,pfe->psqe/dot_general | solution.py:127
  28.2 60.4 %while.13 = (s32[]{:T(128)}, bf16[6,8,96,128]{3,2,1,0:T(8,128)(2,1)}, bf16[6,16,8,96]{3,1,2,0:T(8,128)(2,1)}, s32[6]{0:T(128)S(1)}, bf16[48,96,128]{2,1,0:T(8,12...) while((s32[]{:T(128)}, ...), condition=%wide.region_10.11_spmd.clone, body=%wide.region_0.10_spmd.clone.sunk | while | flops 390749440 | bytes 15165903 | solution.py:118
  31.4 1.1 fusion.91
  35.6 1.0 bitcast_dynamic-update-slice_fusion.2
  37.2 1.0 fusion.96
  41.5 1.1 fusion.91
  45.7 1.0 bitcast_dynamic-update-slice_fusion.2
  47.3 1.0 fusion.96
  51.6 1.1 fusion.91
  55.7 1.0 bitcast_dynamic-update-slice_fusion.2
  57.4 1.0 fusion.96
  61.6 1.1 fusion.91
  65.8 1.0 bitcast_dynamic-update-slice_fusion.2
  67.4 1.0 fusion.96
  71.7 1.1 fusion.91
  75.9 1.0 bitcast_dynamic-update-slice_fusion.2
  81.8 1.1 fusion.91
  85.9 1.0 bitcast_dynamic-update-slice_fusion.2
  88.6 1.7 %copy.48 = bf16[16,6,8,96]{3,2,1,0:T(8,128)(2,1)} copy(bf16[16,6,8,96]{3,0,2,1:T(8,128)(2,1)} %bitcast.136) | data formatting | bytes 294912 | tf_op jit(solution)/shard_map/transpose | solution.py:120
  90.3 4.0 %all-to-all-start = ((bf16[16,48,96]{2,1,0:T(8,128)(2,1)}), bf16[16,48,96]{2,1,0:T(8,128)(2,1)}, u32[]{:S(2)}, u32[]{:S(2)}) async-start(bf16[16,48,96]{2,1,0:T(8,128)(2,1)} %bitcast.106), calls=%async_computation | async-start | bytes 393216 | tf_op jit(solution)/shard_map/all_to_all | solution.py:137
  96.3 3.3 %all-to-all-done = bf16[16,48,96]{2,1,0:T(8,128)(2,1)} async-done(((bf16[16,48,96]{2,1,0:T(8,128)(2,1)}), bf16[16,48,96]{2,1,0:T(8,128)(2,1)}, u32[]{:S(2)}, u32[]{:S(2)}) %all-to-all-start) | async-done | bytes 147488 | tf_op jit(solution)/shard_map/all_to_all | solution.py:137
  101.8 3.4 %fusion.68 = (bf16[8,1,192,384]{2,3,0,1:T(8,128)(2,1)S(1)}, bf16[8,1,192,384]{2,3,0,1:T(8,128)(2,1)}) fusion(bf16[8,2,192,384]{2,3,0,1:T(8,128)(2,1)} %all-gather.2.cloned.1.call-done), kind=kLoop, calls=%fused_computation.116 | loop fusion | bytes 4718592 | tf_op jit(solution)/shard_map/slice | solution.py:139
  105.1 2.5 %copy.27 = bf16[8,1,192,384]{3,2,0,1:T(8,128)(2,1)} copy(bf16[8,1,192,384]{2,3,0,1:T(8,128)(2,1)} %get-tuple-element.183) | data formatting | bytes 2359296 | tf_op jit(solution)/shard_map/slice | solution.py:140
  107.7 1.5 %copy.28 = bf16[8,1,192,384]{3,2,0,1:T(8,128)(2,1)} copy(bf16[8,1,192,384]{2,3,0,1:T(8,128)(2,1)S(1)} %get-tuple-element.182) | data formatting | bytes 2359296 | tf_op jit(solution)/shard_map/slice | solution.py:139
  109.2 3.6 %fusion.71 = (f32[8,4,48]{2,1,0:T(4,128)S(1)}, f32[8,4,48,384]{3,2,1,0:T(8,128)}) fusion(f32[4,48,384]{2,1,0:T(8,128)} %reshape.365, bf16[8,4,48,384]{3,2,1,0:T(8,128)(2,1)} %bitcast.135, bf16[8,48,4,48]{3,2,1,0:T(4,128)(2,1)S(1)} %copy-done.5), kind=kOutput, calls=%fused_computation.119 | convolution fusion | flops 58982784 | bytes 3987456 | tf_op jit(solution)/shard_map/sub | solution.py:72
  112.8 2.3 %convolution_bitcast_fusion.1 = f32[8,48,4,48]{1,3,2,0:T(8,128)S(1)} fusion(bf16[8,4,48,384]{3,2,1,0:T(8,128)(2,1)S(1)} %bitcast.134, f32[8,4,48,384]{3,2,1,0:T(8,128)} %get-tuple-element.190, f32[8,4,48]{2,1,0:T(4,128)S(1)} %get-tuple-element.189), kind=kOutput, calls=%fused_computation.93 | convolution fusion | flops 57802752 | bytes 3840000 | tf_op jit(solution)/shard_map/shqk,shdk->sqhd/dot_general | solution.py:147
  116.5 1.1 copy.35
  117.6 22.5 %reduce-scatter.4.cloned.1.call-done = bf16[192,384]{1,0:T(8,128)(2,1)} async-done(((bf16[768,384]{1,0:T(8,128)(2,1)}), bf16[192,384]{1,0:T(8,128)(2,1)}) %reduce-scatter.4.cloned.1.call-update) | async-done | bytes 147472
  140.1 1.7 %copy.36 = bf16[192,384]{0,1:T(8,128)(2,1)} copy(bf16[192,384]{1,0:T(8,128)(2,1)} %reduce-scatter.4.cloned.1.call-done) | data formatting | bytes 294912
  (236 shorter events, 46.4 us)
Async XLA Ops:
  7.2 17.3 %copy-start = (bf16[4,768,192]{1,2,0:T(8,128)(2,1)S(1)}, bf16[4,768,192]{1,2,0:T(8,128)(2,1)}, u32[]{:S(2)}) copy-start(bf16[4,768,192]{1,2,0:T(8,128)(2,1)} %param.26) | copy-start | bytes 3538948
  7.2 94.6 %all-gather.2.cloned.1.call-start = ((), (), s32[]{:S(2)}) async-start(), calls=%async_computation.2 | async-start | bytes 3538944 | tf_op jit(solution)/shard_map/all_gather | solution.py:138
  26.3 1.7 %copy-start.9 = (s32[3,384]{1,0:T(4,128)S(1)}, s32[3,384]{1,0:T(4,128)}, u32[]{:S(2)}) copy-start(s32[3,384]{1,0:T(4,128)} %param.16) | copy-start | bytes 13828
  26.3 1.8 %copy-start.1 = (bf16[2,128,512]{2,1,0:T(8,128)(2,1)S(1)}, bf16[2,128,512]{2,1,0:T(8,128)(2,1)}, u32[]{:S(2)}) copy-start(bf16[2,128,512]{2,1,0:T(8,128)(2,1)} %param.21) | copy-start | bytes 786436
  26.4 1.8 %copy-start.7 = (bf16[128,16]{0,1:T(8,128)(2,1)S(1)}, bf16[128,16]{0,1:T(8,128)(2,1)}, u32[]{:S(2)}) copy-start(bf16[128,16]{0,1:T(8,128)(2,1)} %param.24) | copy-start | bytes 12292
  26.4 1.8 %copy-start.8 = (f32[2,128]{1,0:T(2,128)S(1)}, f32[2,128]{1,0:T(2,128)}, u32[]{:S(2)}) copy-start(f32[2,128]{1,0:T(2,128)} %param.20) | copy-start | bytes 3076
  26.4 1.7 %copy-start.10 = (f32[128]{0:T(128)S(1)}, f32[128]{0:T(128)}, u32[]{:S(2)}) copy-start(f32[128]{0:T(128)} %param.23) | copy-start | bytes 1540
  26.4 1.7 %copy-start.12 = (bf16[256,128]{1,0:T(8,128)(2,1)S(1)}, bf16[256,128]{1,0:T(8,128)(2,1)}, u32[]{:S(2)}) copy-start(bf16[256,128]{1,0:T(8,128)(2,1)} %param.19) | copy-start | bytes 196612
  26.4 1.7 %copy-start.13 = (bf16[139,128]{1,0:T(8,128)(2,1)S(1)}, bf16[139,128]{1,0:T(8,128)(2,1)}, u32[]{:S(2)}) copy-start(bf16[139,128]{1,0:T(8,128)(2,1)} %param.17) | copy-start | bytes 106756
  26.4 1.7 %copy-start.14 = (f32[256]{0:T(256)S(1)}, f32[256]{0:T(256)}, u32[]{:S(2)}) copy-start(f32[256]{0:T(256)} %param.18) | copy-start | bytes 3076
  33.5 0.9 copy-start.11
  43.5 0.9 copy-start.11
  53.6 0.9 copy-start.11
  63.7 0.9 copy-start.11
  73.7 0.9 copy-start.11
  83.8 0.9 copy-start.11
  88.6 5.9 %copy-start.4 = (bf16[1,8,48,192]{3,2,1,0:T(8,128)(2,1)S(1)}, bf16[1,8,48,192]{3,2,1,0:T(8,128)(2,1)}, u32[]{:S(2)}) copy-start(bf16[1,8,48,192]{3,2,1,0:T(8,128)(2,1)} %get-tuple-element.184) | copy-start | bytes 442372
  90.3 9.4 %all-to-all-start = ((bf16[16,48,96]{2,1,0:T(8,128)(2,1)}), bf16[16,48,96]{2,1,0:T(8,128)(2,1)}, u32[]{:S(2)}, u32[]{:S(2)}) async-start(bf16[16,48,96]{2,1,0:T(8,128)(2,1)} %bitcast.106), calls=%async_computation | async-start | bytes 393216 | tf_op jit(solution)/shard_map/all_to_all | solution.py:137
  94.3 45.9 %reduce-scatter.4.cloned.1.call-start = ((), (), s32[]{:S(2)}) async-start(), calls=%async_computation.3 | async-start | bytes 737280
  107.7 1.5 %copy-start.5 = (bf16[8,48,4,48]{3,2,1,0:T(4,128)(2,1)S(1)}, bf16[8,48,4,48]{3,2,1,0:T(4,128)(2,1)}, u32[]{:S(2)}) copy-start(bf16[8,48,4,48]{3,2,1,0:T(4,128)(2,1)} %convert_element_type.75) | copy-start | bytes 442372
  109.2 3.7 %copy-start.2 = (bf16[8,1,192,384]{3,2,0,1:T(8,128)(2,1)S(1)}, bf16[8,1,192,384]{3,2,0,1:T(8,128)(2,1)}, u32[]{:S(2)}) copy-start(bf16[8,1,192,384]{3,2,0,1:T(8,128)(2,1)} %copy.27) | copy-start | bytes 3538948
  115.1 1.0 copy-start.3
  115.1 1.1 copy-start.6
Sparse Core Ops, SparseCore 0:
  28.1 60.9 all-gather.1
  117.7 22.3 reduce-scatter.3
where the time goes:
time: 150 us; the launch traced here: 149 us
  matrix products  36 us (24%)
  waiting for transfers between devices  25.9 us (17%)
  other arithmetic  24.9 us (17%)
  local copies, waits for them, and re-layouts  24.6 us (16%)
  blocking collectives  14.3 us (10%)
  between operations  14.3 us (10%)
  loops' own time  4.55 us (3%)
  starting transfers between devices  4.06 us (3%)
    unnamed x3, waiting for transfers between devices  22.6 us
    all_gather x1, blocking collectives, shards(): lax.all_gather(normed, 'ka', axis=2, tiled=True)  14.3 us
    dot_general x12, matrix products, condition_block(): jnp.einsum('rkf,fc->rkc', hidden, trans_out[layer_idx], preferred_element...  8.85 us
    reduce_sum x24, other arithmetic, layer_norm(): spread = jnp.mean(centered * centered, axis=-1, keepdims=True)  8.37 us
    reduce_sum x12, other arithmetic, layer_norm(): average = jnp.mean(values, axis=-1, keepdims=True)  7.67 us
    dot_general x6, matrix products, condition_block(): jnp.einsum('rkc,ch->hrk', normal_b, w_bias, preferred_element_type=jnp.fl...  6.08 us
    convert_element_type x6, other arithmetic, condition_block(): joined = jnp.concatenate([trunk_blk.astype(jnp.float32), relative], axis=-1)  5.75 us
    dot_general x12, matrix products, condition_block(): jnp.einsum('rkc,cf->rkf', normal_tr, trans_ab[layer_idx], preferred_eleme...  5.08 us
  transfers between devices with their start and end apart: 3, of which 2 were waited for; matrix products, arithmetic and copies ran while one was open for 41% of the time, Pallas kernels for 0%

commit v1 on v0

--- a/solution.py
+++ b/solution.py
@@ -9,6 +9,22 @@
 SMAX = 2
 REL = 139
 EPS = 1e-05
+
+
+def ring_product(x, axis, dim, contribution):
+    size, index, width = (lax.axis_size(axis), lax.axis_index(axis), x.shape[dim])
+    right = [(i, (i + 1) % size) for i in range(size)]
+    backward = [(i, (i - 1) % size) for i in range(size)]
+    half = size // 2
+    from_left = from_right = x
+    running = contribution(x, index * width)
+    for step in range(1, half + 1):
+        from_left = lax.ppermute(from_left, axis, right)
+        if step < size - half:
+            from_right = lax.ppermute(from_right, axis, backward)
+            running = running + contribution(from_right, (index + step) % size * width)
+        running = running + contribution(from_left, (index - step) % size * width)
+    return running
 
 
 def layer_norm(values, scaling):
@@ -124,11 +140,16 @@
     feat_local = normed.shape[2]
     heads_local = feat_local // HD
     scale_factor = 1.0 / math.sqrt(HD)
-    projected = jnp.einsum(
-        "sqf,pfe->psqe",
-        lax.all_gather(normed, "ka", axis=2, tiled=True),
-        w_proj,
-        preferred_element_type=jnp.float32,
+    projected = ring_product(
+        normed,
+        "ka",
+        2,
+        lambda shard, offset: jnp.einsum(
+            "sqf,pfe->psqe",
+            shard,
+            lax.dynamic_slice_in_dim(w_proj, offset, shard.shape[2], axis=1),
+            preferred_element_type=jnp.float32,
+        ),
     )
     queries = projected[0].astype(jnp.bfloat16).reshape(samples, q_rows, heads_local, HD)
     kv_local = jnp.transpose(

time: 150 us -> 138 us (0.920)
  local copies, waits for them, and re-layouts: 24.6 us -> 17.2 us
  blocking collectives: 14.3 us -> 10.7 us
    all_gather x1 -> x0, blocking collectives: 14.3 us -> none  [shards(): lax.all_gather(normed, 'ka', axis=2, tiled=True)]
    all_to_all x0 -> x1, blocking collectives: none -> 10.7 us  [shards(): lax.all_to_all(bias_tile, 'ka', split_axis=0, concat_axis=2, tiled=True)]
    ppermute x0 -> x3, starting transfers between devices: none -> 4.59 us  [the longest x2 2.61 us: ring_product(): from_left = lax.ppermute(from_left, axis, right)]
    all_to_all x1 -> x0, starting transfers between devices: 3.99 us -> none  [shards(): lax.all_to_all(bias_tile, 'ka', split_axis=0, concat_axis=2, tiled=True)]
    ppermute x0 -> x3, waiting for transfers between devices: none -> 3.97 us  [the longest x2 3.97 us: ring_product(): from_left = lax.ppermute(from_left, axis, right)]
    dot_general x6, matrix products: 6.08 us -> 2.41 us  [condition_block(): jnp.einsum('rkc,ch->hrk', normal_b, w_bias, preferred_element_type=jnp.fl...]
    all_to_all x1 -> x0, waiting for transfers between devices: 3.34 us -> none  [shards(): lax.all_to_all(bias_tile, 'ka', split_axis=0, concat_axis=2, tiled=True)]
    dot_general x1 -> x4, matrix products: 1.85 us -> 4.06 us  [shards(): jnp.einsum('sqf,pfe->psqe', shard, lax.dynamic_slice_in_dim(w_proj, offse...]
  transfers between devices with their start and end apart: 3 -> 5, of which waited for: 2 -> 3; matrix products, arithmetic and copies ran while one was open for 41% -> 41% of each run, Pallas kernels for 0% -> 0%
where the time goes in v1:
time: 138 us; the launch traced here: 137 us
  matrix products  34.6 us (25%)
  waiting for transfers between devices  25.8 us (19%)
  other arithmetic  25 us (18%)
  local copies, waits for them, and re-layouts  17.2 us (12%)
  between operations  14.4 us (10%)
  blocking collectives  10.7 us (8%)
  loops' own time  5 us (4%)
  starting transfers between devices  4.67 us (3%)
    unnamed x3, waiting for transfers between devices  21.8 us
    all_to_all x1, blocking collectives, shards(): lax.all_to_all(bias_tile, 'ka', split_axis=0, concat_axis=2, tiled=True)  10.7 us
    dot_general x12, matrix products, condition_block(): jnp.einsum('rkf,fc->rkc', hidden, trans_out[layer_idx], preferred_element...  8.82 us
    reduce_sum x24, other arithmetic, layer_norm(): spread = jnp.mean(centered * centered, axis=-1, keepdims=True)  8.34 us
    reduce_sum x12, other arithmetic, layer_norm(): average = jnp.mean(values, axis=-1, keepdims=True)  7.67 us
    convert_element_type x6, other arithmetic, condition_block(): joined = jnp.concatenate([trunk_blk.astype(jnp.float32), relative], axis=-1)  5.79 us
    dot_general x12, matrix products, condition_block(): jnp.einsum('rkc,cf->rkf', normal_tr, trans_ab[layer_idx], preferred_eleme...  5.08 us
    another operation x1, loops' own time, shards(): lax.map(one_block, jnp.arange(q_rows // row_blk, dtype=jnp.int32))  5 us
  transfers between devices with their start and end apart: 5, of which 3 were waited for; matrix products, arithmetic and copies ran while one was open for 41% of the time, Pallas kernels for 0%

profile of v1, /device:TPU:0, one launch (start us, length us, event | category | flops | bytes accessed | tf_op | source)
XLA Modules:
  0.0 137.3 jit_solution(17144196762787633392)
XLA Ops:
  7.8 2.0 %collective-permute-start = (bf16[8,48,192]{2,1,0:T(8,128)(2,1)}, bf16[8,48,192]{2,1,0:T(8,128)(2,1)S(1)}, u32[]{:S(2)}, u32[]{:S(2)}) collective-permute-start(bf16[8,48,192]{2,1,0:T(8,128)(2,1)} %param.25), channel_id=1, source_target_pairs={{0,3},{1,0},{2,1},{3,2},{4,7},{5,4},{6,5},{7,6},{8,11},{9,8},{10,9... | collective-permute-start | bytes 442376 | tf_op jit(solution)/shard_map/ppermute | solution.py:24
  9.8 1.4 %fusion.59 = f32[4,192,8,48]{1,3,2,0:T(8,128)S(1)} fusion(bf16[4,768,192]{1,2,0:T(8,128)(2,1)S(1)} %copy-done, s32[]{:T(128)S(6)} %select_n.59, bf16[8,48,192]{2,1,0:T(8,128)(2,1)} %param.25), kind=kOutput, calls=%fused_computation.107 | convolution fusion | flops 113246208 | bytes 1720324 | tf_op jit(solution)/shard_map/sqf,pfe->psqe/dot_general | solution.py:147
  11.4 1.9 %collective-permute-done.1 = bf16[8,48,192]{2,1,0:T(8,128)(2,1)S(1)} collective-permute-done((bf16[8,48,192]{2,1,0:T(8,128)(2,1)}, bf16[8,48,192]{2,1,0:T(8,128)(2,1)S(1)}, u32[]{:S(2)}, u32[]{:S(2)}) %collective-permute-start.1) | collective-permute-done | bytes 147488 | tf_op jit(solution)/shard_map/ppermute | solution.py:22
  13.3 2.1 %collective-permute-start.2 = (bf16[8,48,192]{2,1,0:T(8,128)(2,1)S(1)}, bf16[8,48,192]{2,1,0:T(8,128)(2,1)S(1)}, u32[]{:S(2)}, u32[]{:S(2)}) collective-permute-start(bf16[8,48,192]{2,1,0:T(8,128)(2,1)S(1)} %collective-permute-done.1), channel_id=1, source_target_pairs={{0,1},{1,2},{2,3},{3,0},{4,5},{5,6},{6,7},{7,4},{8,9},{9,10},{10,1... | collective-permute-start | bytes 442376 | tf_op jit(solution)/shard_map/ppermute | solution.py:22
  16.3 2.1 %collective-permute-done.2 = bf16[8,48,192]{2,1,0:T(8,128)(2,1)S(1)} collective-permute-done((bf16[8,48,192]{2,1,0:T(8,128)(2,1)S(1)}, bf16[8,48,192]{2,1,0:T(8,128)(2,1)S(1)}, u32[]{:S(2)}, u32[]{:S(2)}) %collective-permute-start.2) | collective-permute-done | bytes 147488 | tf_op jit(solution)/shard_map/ppermute | solution.py:22
  18.4 1.7 %fusion.87 = (bf16[4,8,48,192]{3,2,1,0:T(8,128)(2,1)S(1)}, f32[4,8,48,192]{3,2,1,0:T(8,128)}) fusion(bf16[8,48,192]{2,1,0:T(8,128)(2,1)S(1)} %collective-permute-done.2, bf16[4,768,192]{1,2,0:T(8,128)(2,1)S(1)} %copy-done, s32[]{:T(128)S(6)} %select_n.65, f32[4,192,8,48]{1,3,2,0:T(8,128)S(1)} %fusion.55, f32[4,192,8,48]{1,3,2,0:T(8,128)S(1)} %fusion.59, ...), kind=kOutput, calls=%fused_computation.135 | convolution fusion | flops 114425856 | bytes 7077892 | tf_op jit(solution)/shard_map/sqf,pfe->psqe/dot_general | solution.py:147
  21.2 56.7 %while.13 = (s32[]{:T(128)}, bf16[6,8,96,128]{3,2,1,0:T(8,128)(2,1)}, bf16[6,16,8,96]{3,1,2,0:T(8,128)(2,1)S(1)}, s32[6]{0:T(128)S(1)}, bf16[48,96,128]{2,1,0:T(...) while((s32[]{:T(128)}, ...), condition=%wide.region_10.11_spmd.clone, body=%wide.region_0.10_spmd.clone.sunk | while | flops 390749440 | bytes 14643635 | solution.py:134
  24.5 1.1 fusion.108
  28.6 1.0 bitcast_dynamic-update-slice_fusion.2
  33.0 1.0 dynamic-slice_convert_fusion.2
  34.0 1.1 fusion.108
  38.0 1.0 bitcast_dynamic-update-slice_fusion.2
  42.5 1.0 dynamic-slice_convert_fusion.2
  43.4 1.1 fusion.108
  47.5 1.0 bitcast_dynamic-update-slice_fusion.2
  52.9 1.1 fusion.108
  56.9 1.0 bitcast_dynamic-update-slice_fusion.2
  61.4 1.0 dynamic-slice_convert_fusion.2
  62.3 1.1 fusion.108
  66.4 1.0 bitcast_dynamic-update-slice_fusion.2
  71.8 1.1 fusion.108
  75.8 1.0 bitcast_dynamic-update-slice_fusion.2
  77.9 10.7 %all_to_all.4 = bf16[16,48,96]{2,1,0:T(8,128)(2,1)S(1)} all-to-all(bf16[16,48,96]{2,1,0:T(8,128)(2,1)S(1)} %bitcast.164), channel_id=1, replica_groups=mesh['pb'=8,'ka'=4] {'ka'}, dimensions={0} | all-to-all | bytes 294912 | tf_op jit(solution)/shard_map/all_to_all | solution.py:158
  90.1 1.1 fusion.53
  91.4 3.3 %fusion.85 = (bf16[8,1,192,384]{2,3,0,1:T(8,128)(2,1)S(1)}, bf16[8,1,192,384]{2,3,0,1:T(8,128)(2,1)}) fusion(bf16[8,2,192,384]{2,3,0,1:T(8,128)(2,1)} %all-gather.2.cloned.1.call-done), kind=kLoop, calls=%fused_computation.133 | loop fusion | bytes 4718592 | tf_op jit(solution)/shard_map/slice | solution.py:160
  94.6 2.5 %copy.37 = bf16[8,1,192,384]{3,2,0,1:T(8,128)(2,1)} copy(bf16[8,1,192,384]{2,3,0,1:T(8,128)(2,1)} %get-tuple-element.183) | data formatting | bytes 2359296 | tf_op jit(solution)/shard_map/slice | solution.py:161
  97.1 1.5 %copy.38 = bf16[8,1,192,384]{3,2,0,1:T(8,128)(2,1)} copy(bf16[8,1,192,384]{2,3,0,1:T(8,128)(2,1)S(1)} %get-tuple-element.182) | data formatting | bytes 2359296 | tf_op jit(solution)/shard_map/slice | solution.py:160
  98.6 3.7 %fusion.88 = (f32[8,4,48]{2,1,0:T(4,128)S(1)}, f32[8,4,48,384]{3,2,1,0:T(8,128)}) fusion(f32[4,48,384]{2,1,0:T(8,128)} %reshape.365, bf16[8,4,48,384]{3,2,1,0:T(8,128)(2,1)} %bitcast.163, bf16[8,48,4,48]{3,2,1,0:T(4,128)(2,1)S(1)} %convert_element_type.75), kind=kOutput, calls=%fused_computation.136 | convolution fusion | flops 58982784 | bytes 3987456 | tf_op jit(solution)/shard_map/sub | solution.py:88
  102.3 2.3 %convolution_bitcast_fusion = f32[8,48,4,48]{1,3,2,0:T(8,128)S(1)} fusion(bf16[8,4,48,384]{3,2,1,0:T(8,128)(2,1)S(1)} %bitcast.162, f32[8,4,48,384]{3,2,1,0:T(8,128)} %get-tuple-element.190, f32[8,4,48]{2,1,0:T(4,128)S(1)} %get-tuple-element.189), kind=kOutput, calls=%fused_computation.93 | convolution fusion | flops 57802752 | bytes 3840000 | tf_op jit(solution)/shard_map/shqk,shdk->sqhd/dot_general | solution.py:168
  106.0 1.0 copy.48
  107.0 21.7 %reduce-scatter.4.cloned.1.call-done = bf16[192,384]{1,0:T(8,128)(2,1)} async-done(((bf16[768,384]{1,0:T(8,128)(2,1)}), bf16[192,384]{1,0:T(8,128)(2,1)}) %reduce-scatter.4.cloned.1.call-update) | async-done | bytes 147472
  128.8 1.7 %copy.49 = bf16[192,384]{0,1:T(8,128)(2,1)} copy(bf16[192,384]{1,0:T(8,128)(2,1)} %reduce-scatter.4.cloned.1.call-done) | data formatting | bytes 294912
  (225 shorter events, 41.7 us)
Async XLA Ops:
  7.2 2.6 %copy-start = (bf16[4,768,192]{1,2,0:T(8,128)(2,1)S(1)}, bf16[4,768,192]{1,2,0:T(8,128)(2,1)}, u32[]{:S(2)}) copy-start(bf16[4,768,192]{1,2,0:T(8,128)(2,1)} %param.26) | copy-start | bytes 3538948
  7.2 4.1 %copy-start.6 = (s32[3,384]{1,0:T(4,128)S(1)}, s32[3,384]{1,0:T(4,128)}, u32[]{:S(2)}) copy-start(s32[3,384]{1,0:T(4,128)} %param.16) | copy-start | bytes 13828
  7.2 84.2 %all-gather.2.cloned.1.call-start = ((), (), s32[]{:S(2)}) async-start(), calls=%async_computation.2 | async-start | bytes 3538944 | tf_op jit(solution)/shard_map/all_gather | solution.py:159
  7.2 6.0 %collective-permute-start.1 = (bf16[8,48,192]{2,1,0:T(8,128)(2,1)}, bf16[8,48,192]{2,1,0:T(8,128)(2,1)S(1)}, u32[]{:S(2)}, u32[]{:S(2)}) collective-permute-start(bf16[8,48,192]{2,1,0:T(8,128)(2,1)} %param.25), channel_id=1, source_target_pairs={{0,1},{1,2},{2,3},{3,0},{4,5},{5,6},{6,7},{7,4},{8,9},{9,10},{10,1... | collective-permute-start | bytes 442376 | tf_op jit(solution)/shard_map/ppermute | solution.py:22
  7.8 8.0 %collective-permute-start = (bf16[8,48,192]{2,1,0:T(8,128)(2,1)}, bf16[8,48,192]{2,1,0:T(8,128)(2,1)S(1)}, u32[]{:S(2)}, u32[]{:S(2)}) collective-permute-start(bf16[8,48,192]{2,1,0:T(8,128)(2,1)} %param.25), channel_id=1, source_target_pairs={{0,3},{1,0},{2,1},{3,2},{4,7},{5,4},{6,5},{7,6},{8,11},{9,8},{10,9... | collective-permute-start | bytes 442376 | tf_op jit(solution)/shard_map/ppermute | solution.py:24
  13.3 5.1 %collective-permute-start.2 = (bf16[8,48,192]{2,1,0:T(8,128)(2,1)S(1)}, bf16[8,48,192]{2,1,0:T(8,128)(2,1)S(1)}, u32[]{:S(2)}, u32[]{:S(2)}) collective-permute-start(bf16[8,48,192]{2,1,0:T(8,128)(2,1)S(1)} %collective-permute-done.1), channel_id=1, source_target_pairs={{0,1},{1,2},{2,3},{3,0},{4,5},{5,6},{6,7},{7,4},{8,9},{9,10},{10,1... | collective-permute-start | bytes 442376 | tf_op jit(solution)/shard_map/ppermute | solution.py:22
  20.0 1.0 copy-start.1
  20.1 1.0 copy-start.4
  20.1 1.0 copy-start.5
  20.1 1.1 copy-start.7
  20.1 1.1 copy-start.8
  20.1 1.1 copy-start.9
  20.1 1.1 copy-start.10
  20.1 1.1 copy-start.11
  21.0 107.8 %reduce-scatter.4.cloned.1.call-start = ((), (), s32[]{:S(2)}) async-start(), calls=%async_computation.3 | async-start | bytes 737280
  98.6 3.7 %copy-start.2 = (bf16[8,1,192,384]{3,2,0,1:T(8,128)(2,1)S(1)}, bf16[8,1,192,384]{3,2,0,1:T(8,128)(2,1)}, u32[]{:S(2)}) copy-start(bf16[8,1,192,384]{3,2,0,1:T(8,128)(2,1)} %copy.37) | copy-start | bytes 3538948
  104.6 1.0 copy-start.3
Sparse Core Ops, SparseCore 0:
  21.1 63.4 all-gather.1
  107.2 21.5 reduce-scatter.3
